TPU v7x, 256 devices: a whole 4x4x8 slice. The times are simulated.
256 devices in a mesh: fibre: 2 (over core), chan: 128 (over z, x, y).
Axes of the slice: x: 4, y: 4, z: 8, core: 2. Of those that a mesh axis runs over, the one named last changes fastest.
Arguments:
- raw: bfloat16 [32768, 4096], P(('fibre', 'chan'))
- starts: int32 [4], replicated, may hold values from 0 to 3072, as said below
- ref_ids: int32 [64], replicated, may hold values from 0 to 32767, as said below
- near_ids: int32 [32768, 8], P(('fibre', 'chan')), may hold values from 0 to 32767, as said below
- cross_ids: int32 [32768, 2], P(('fibre', 'chan')), may hold values from 0 to 255
- cross_mask: int32 [32768, 2], P(('fibre', 'chan')), may hold values 0 or 1
- export_loc: int32 [256], P(('fibre', 'chan')), may hold values from 0 to 127
Outputs:
- correlations: bfloat16 [32768, 64, 512], P(('fibre', 'chan'))
Inputs may be any that keep to these rules, and one draw needn't show every extreme that they name: starts[3] is 3072. `ref_ids`: distinct channel ids. `near_ids`: each neighbour lies on the same route as its channel (route = id // 16384) and at most 16 channels away from it.
All inputs are finite; a program needn't handle non-finite values. No bound on the sum of `cross_mask` on one device may be relied on, other than what follows from the above.
Results may differ from a plain program's by a relative error of at most 0.0063.
The roundings to bfloat16 on the way count: a program that leaves them out, or rounds other values in their place, can miss the bound.
Values may be sent and summed in bfloat16 or wider, within the bound.
A program may use at most 128 MiB of HBM per device.

v0:
```python
import math
import jax
import jax.numpy as jnp
from jax import lax
from jax.sharding import PartitionSpec as P

SEG = 1024
SEGS = 4
REFS = 64
LAGS = 512
NN = 8
HALO = 16


def with_halo(block, sides, width):
    for axis, dim in sides:
        count = lax.axis_size(axis)
        forward = [(i, i + 1) for i in range(count - 1)]
        backward = [(target, source) for source, target in forward]
        low = lax.ppermute(
            lax.slice_in_dim(block, block.shape[dim] - width, None, axis=dim), axis, forward
        )
        high = lax.ppermute(lax.slice_in_dim(block, 0, width, axis=dim), axis, backward)
        block = jnp.concatenate([low, block, high], axis=dim)
    return block


def forward_table():
    nbins = SEG // 2
    sample = jnp.arange(SEG, dtype=jnp.int32)
    freq = jnp.arange(nbins, dtype=jnp.int32)
    phase = jnp.mod(sample[:, None] * freq[None, :], SEG).astype(jnp.float32)
    theta = phase * (2.0 * math.pi / SEG)
    keep = (freq > 0).astype(jnp.float32)[None, :]
    return jnp.concatenate([jnp.cos(theta) * keep, -jnp.sin(theta)], 1).astype(jnp.bfloat16)


def lag_table():
    nbins = SEG // 2
    freq = jnp.arange(nbins, dtype=jnp.int32)
    lag = jnp.arange(LAGS, dtype=jnp.int32) - LAGS // 2
    phase = jnp.mod(freq[:, None] * lag[None, :], SEG).astype(jnp.float32)
    theta = phase * (2.0 * math.pi / SEG)
    scale = 1.0 / math.sqrt(nbins)
    table = jnp.concatenate([jnp.cos(theta) * scale, -jnp.sin(theta) * scale], 0)
    return table.astype(jnp.bfloat16)


def per_device(raw, starts, ref_ids, near_ids, cross_ids, cross_mask, export_loc):
    nbins = SEG // 2
    width = SEGS * SEG
    local_ch = raw.shape[0]
    block_base = lax.axis_index(("fibre", "chan")) * local_ch
    pieces = [lax.dynamic_slice_in_dim(raw, starts[s], SEG, 1) for s in range(SEGS)]
    segment = jnp.stack(pieces, 1)
    spectrum = jnp.dot(
        segment.reshape(local_ch * SEGS, SEG), forward_table(), preferred_element_type=jnp.float32
    )
    power = jnp.sum(spectrum * spectrum, -1, keepdims=True) / nbins
    whitened = (spectrum / jnp.sqrt(power + 1e-06)).astype(jnp.bfloat16)
    flat = whitened.reshape(local_ch, width)
    columns = jnp.arange(local_ch, dtype=jnp.int32)
    pick = (ref_ids[:, None] - block_base == columns[None, :]).astype(jnp.bfloat16)
    selected = jnp.dot(pick, flat, preferred_element_type=jnp.float32)
    references = lax.psum(selected, ("fibre", "chan")).astype(jnp.bfloat16)
    extended = with_halo(flat, (("chan", 0),), HALO)
    ext_rows = local_ch + 2 * HALO
    position = near_ids - (block_base - HALO)
    near_count = jnp.sum(
        (position[:, :, None] == jnp.arange(ext_rows, dtype=jnp.int32)[None, None, :]).astype(
            jnp.float32
        ),
        1,
    )
    total = flat.astype(jnp.float32) + jnp.dot(
        near_count.astype(jnp.bfloat16), extended, preferred_element_type=jnp.float32
    )
    exported = jnp.take(flat, export_loc, axis=0)
    live = cross_mask == 1
    piece = lax.all_gather(exported, ("fibre", "chan"), axis=0, tiled=True)
    slots = jnp.arange(piece.shape[0], dtype=jnp.int32)
    hits = (cross_ids[:, :, None] == slots[None, None, :]) & live[:, :, None]
    weights = jnp.sum(hits.astype(jnp.float32), 1).astype(jnp.bfloat16)
    crossing = jnp.dot(weights, piece, preferred_element_type=jnp.float32)
    count = 1.0 + NN + jnp.sum(cross_mask.astype(jnp.float32), 1)
    smoothed = ((total + crossing) / count[:, None]).astype(jnp.bfloat16)
    kernel = lag_table()
    ref_split = references.reshape(REFS, SEGS, SEG)
    ref_re = ref_split[..., :nbins]
    ref_im = ref_split[..., nbins:]
    group = math.gcd(local_ch, 32)

    def correlate(rows):
        a_re = rows[..., :nbins]
        a_im = rows[..., nbins:]
        g_re = jnp.einsum(
            "csf,rsf->crf", a_re, ref_re, preferred_element_type=jnp.float32
        ) + jnp.einsum("csf,rsf->crf", a_im, ref_im, preferred_element_type=jnp.float32)
        g_im = jnp.einsum(
            "csf,rsf->crf", a_im, ref_re, preferred_element_type=jnp.float32
        ) - jnp.einsum("csf,rsf->crf", a_re, ref_im, preferred_element_type=jnp.float32)
        cross = (jnp.concatenate([g_re, g_im], -1) / SEGS).astype(jnp.bfloat16)
        out = jnp.dot(cross.reshape(group * REFS, SEG), kernel, preferred_element_type=jnp.float32)
        return out.astype(jnp.bfloat16).reshape(group, REFS, LAGS)

    result = lax.map(correlate, smoothed.reshape(local_ch // group, group, SEGS, SEG))
    return result.reshape(local_ch, REFS, LAGS)


def solution(mesh):
    in_specs = (
        P(("fibre", "chan"), None),
        P(),
        P(),
        P(("fibre", "chan"), None),
        P(("fibre", "chan"), None),
        P(("fibre", "chan"), None),
        P(("fibre", "chan")),
    )
    out_specs = P(("fibre", "chan"), None, None)
    return jax.shard_map(
        per_device, mesh=mesh, in_specs=in_specs, out_specs=out_specs, check_vma=False
    )
```

profile of v0, /device:TPU:1, one launch (start us, length us, event | category | flops | bytes accessed | tf_op | source)
XLA Modules:
  0.0 315.5 jit_solution(655089644088672558)
XLA Ops:
  6.5 1.5 fusion.53
  13.1 8.0 %negate_convert_fusion = bf16[1024,512]{1,0:T(8,128)(2,1)S(1)} fusion(), kind=kLoop, calls=%fused_computation.36 | loop fusion | flops 8388608 | bytes 1048576 | tf_op jit(solution)/shard_map/convert.3
  23.6 1.9 dynamic-slice_bitcast_fusion.3
  25.6 0.8 copy.42
  26.4 0.3 reshape.58
  26.7 7.9 %multiply_convert_fusion = bf16[1024,512]{1,0:T(8,128)(2,1)S(1)} fusion(f32[512]{0:T(512)S(1)} %fusion.48), kind=kLoop, calls=%fused_computation.37 | loop fusion | flops 8388608 | bytes 1050624 | tf_op jit(solution)/shard_map/convert.2
  34.7 1.3 multiply_reduce_fusion
  36.0 0.3 divide_convert_fusion
  36.3 0.7 reshape.59
  37.7 0.6 fusion.46
  38.5 4.0 %collective-permute-start = (bf16[16,4096]{1,0:T(8,128)(2,1)S(1)}, bf16[16,4096]{1,0:T(8,128)(2,1)S(1)}, u32[]{:S(2)}, u32[]{:S(2)}) collective-permute-start(bf16[16,4096]{1,0:T(8,128)(2,1)S(1)} %slice.41), channel_id=1, source_target_pairs={{0,1},{1,2},{2,3},{3,4},{4,5},{5,6},{6,7},{7,8},{8,9},{9,10},{10,1... | collective-permute-start | bytes 393224 | tf_op jit(solution)/shard_map/ppermute | solution.py:20
  42.6 1.3 collective-permute-start.1
  43.9 0.3 fusion.45
  44.3 88.9 %all-reduce.1 = bf16[64,4096]{1,0:T(8,128)(2,1)S(1)} all-reduce(f32[64,4096]{1,0:T(8,128)S(1)} %fusion.45), channel_id=1, replica_groups=mesh['fibre'=2,'chan'=128] {'fibre','chan'}, use_global_device_ids=true, to_apply=%region_4.5 | all-reduce | flops 262144 | bytes 1572864 | tf_op jit(solution)/shard_map/psum | solution.py:65
  133.2 0.4 reshape.61
  133.8 1.1 copy.48
  134.9 1.1 copy.49
  136.3 4.5 %multiply_convert_fusion.2 = (bf16[512,512]{1,0:T(8,128)(2,1)S(1)}, bf16[512,512]{1,0:T(8,128)(2,1)S(1)}) fusion(s32[512]{0:T(512)S(1)} %iota_add_fusion), kind=kLoop, calls=%fused_computation.55 | loop fusion | flops 4980736 | bytes 1050624 | tf_op jit(solution)/shard_map/convert
  140.8 1.0 pad_maximum_fusion.1
  141.9 16.6 %all-gather.3.cloned.1.call-done = bf16[256,1,4096]{2,1,0:T(2,128)(2,1)} async-done(((bf16[1,1,4096]{2,1,0:T(2,128)(2,1)}), bf16[256,1,4096]{2,1,0:T(2,128)(2,1)}) %all-gather.3.cloned.1.call-update) | async-done | bytes 2097168 | tf_op jit(solution)/shard_map/all_gather | solution.py:80
  158.5 4.7 %fusion.25 = f32[128,4096]{1,0:T(8,128)S(1)} fusion(bf16[256,1,4096]{2,1,0:T(2,128)(2,1)} %all-gather.3.cloned.1.call-done, bf16[128,256]{1,0:T(8,128)(2,1)S(1)} %convert_reduce_fusion.1), kind=kOutput, calls=%fused_computation.31 | convolution fusion | flops 268435456 | bytes 4259840 | tf_op jit(solution)/shard_map/dot_general | solution.py:84
  163.2 0.6 fusion.17
  163.8 0.8 reshape.60
  164.9 143.8 %while.11 = (s32[]{:T(128)}, bf16[4,32,64,512]{3,2,1,0:T(8,128)(2,1)}, bf16[4,32,4,1024]{3,2,1,0:T(4,128)(2,1)S(1)}, bf16[64,4,512]{0,1,2:T(4,128)(2,1)S(1)}, bf...) while((s32[]{:T(128)}, ...), condition=%wide.region_6.7_spmd, body=%wide.region_5.6_spmd.sunk | while | flops 2190475264 | bytes 77595424 | solution.py:106
  164.9 1.0 copy-done
  166.0 0.8 copy.57
  166.8 1.3 fusion.87
  168.1 4.9 %add_bitcast_fusion.2 = f32[32,64,512]{1,0,2:T(8,128)} fusion(f32[512,32,64]{2,1,0:T(8,128)S(1)} %fusion.87, bf16[64,4,512]{0,1,2:T(4,128)(2,1)S(1)} %copy-done.6, bf16[1,32,4,1024]{1,2,3,0:T(4,128)(2,1)S(1)} %copy.57), kind=kOutput, calls=%fused_computation.3.clone.1 | convolution fusion | flops 9437184 | bytes 8912896 | tf_op jit(solution)/shard_map/while/body/eval_jaxpr/csf,rsf->crf/dot_general | solution.py:98
  173.1 6.9 %copy.59 = f32[32,64,512]{2,1,0:T(8,128)} copy(f32[32,64,512]{1,0,2:T(8,128)} %add_bitcast_fusion.2) | data formatting | bytes 8388608 | tf_op jit(solution)/shard_map/while/body/eval_jaxpr/add | solution.py:96
  180.0 1.3 fusion.86
  181.3 4.9 %subtract_bitcast_fusion.2 = f32[32,64,512]{1,0,2:T(8,128)} fusion(f32[512,32,64]{2,1,0:T(8,128)S(1)} %fusion.86, bf16[64,4,512]{0,1,2:T(4,128)(2,1)S(1)} %copy-done.7, bf16[1,32,4,1024]{1,2,3,0:T(4,128)(2,1)S(1)} %copy.57), kind=kOutput, calls=%fused_computation.2.clone.1 | convolution fusion | flops 9437184 | bytes 8912896 | tf_op jit(solution)/shard_map/while/body/eval_jaxpr/csf,rsf->crf/dot_general | solution.py:101
  186.2 6.9 %copy.58 = f32[32,64,512]{2,1,0:T(8,128)} copy(f32[32,64,512]{1,0,2:T(8,128)} %subtract_bitcast_fusion.2) | data formatting | bytes 8388608 | tf_op jit(solution)/shard_map/while/body/eval_jaxpr/sub | solution.py:99
  193.2 5.8 %fusion.88 = bf16[2048,512]{1,0:T(8,128)(2,1)S(1)} fusion(bf16[1024,512]{1,0:T(8,128)(2,1)S(1)} %copy-done.2, f32[2048,512]{1,0:T(8,128)} %bitcast.74, f32[2048,512]{1,0:T(8,128)} %bitcast.73), kind=kOutput, calls=%fused_computation.6.clone.1 | convolution fusion | flops 2154823680 | bytes 11534336 | tf_op jit(solution)/shard_map/while/body/eval_jaxpr/dot_general | solution.py:103
  199.0 1.6 constant_dynamic-update-slice_fusion.2
  200.8 1.0 copy-done
  202.0 0.8 copy.57
  202.7 1.3 fusion.87
  204.1 4.9 %add_bitcast_fusion.2 = f32[32,64,512]{1,0,2:T(8,128)} fusion(f32[512,32,64]{2,1,0:T(8,128)S(1)} %fusion.87, bf16[64,4,512]{0,1,2:T(4,128)(2,1)S(1)} %copy-done.6, bf16[1,32,4,1024]{1,2,3,0:T(4,128)(2,1)S(1)} %copy.57), kind=kOutput, calls=%fused_computation.3.clone.1 | convolution fusion | flops 9437184 | bytes 8912896 | tf_op jit(solution)/shard_map/while/body/eval_jaxpr/csf,rsf->crf/dot_general | solution.py:98
  209.0 6.9 %copy.59 = f32[32,64,512]{2,1,0:T(8,128)} copy(f32[32,64,512]{1,0,2:T(8,128)} %add_bitcast_fusion.2) | data formatting | bytes 8388608 | tf_op jit(solution)/shard_map/while/body/eval_jaxpr/add | solution.py:96
  215.9 1.3 fusion.86
  217.2 4.9 %subtract_bitcast_fusion.2 = f32[32,64,512]{1,0,2:T(8,128)} fusion(f32[512,32,64]{2,1,0:T(8,128)S(1)} %fusion.86, bf16[64,4,512]{0,1,2:T(4,128)(2,1)S(1)} %copy-done.7, bf16[1,32,4,1024]{1,2,3,0:T(4,128)(2,1)S(1)} %copy.57), kind=kOutput, calls=%fused_computation.2.clone.1 | convolution fusion | flops 9437184 | bytes 8912896 | tf_op jit(solution)/shard_map/while/body/eval_jaxpr/csf,rsf->crf/dot_general | solution.py:101
  222.2 6.9 %copy.58 = f32[32,64,512]{2,1,0:T(8,128)} copy(f32[32,64,512]{1,0,2:T(8,128)} %subtract_bitcast_fusion.2) | data formatting | bytes 8388608 | tf_op jit(solution)/shard_map/while/body/eval_jaxpr/sub | solution.py:99
  229.1 5.8 %fusion.88 = bf16[2048,512]{1,0:T(8,128)(2,1)S(1)} fusion(bf16[1024,512]{1,0:T(8,128)(2,1)S(1)} %copy-done.2, f32[2048,512]{1,0:T(8,128)} %bitcast.74, f32[2048,512]{1,0:T(8,128)} %bitcast.73), kind=kOutput, calls=%fused_computation.6.clone.1 | convolution fusion | flops 2154823680 | bytes 11534336 | tf_op jit(solution)/shard_map/while/body/eval_jaxpr/dot_general | solution.py:103
  235.0 1.6 constant_dynamic-update-slice_fusion.2
  236.8 1.0 copy-done
  237.9 0.8 copy.57
  238.7 1.3 fusion.87
  240.0 4.9 %add_bitcast_fusion.2 = f32[32,64,512]{1,0,2:T(8,128)} fusion(f32[512,32,64]{2,1,0:T(8,128)S(1)} %fusion.87, bf16[64,4,512]{0,1,2:T(4,128)(2,1)S(1)} %copy-done.6, bf16[1,32,4,1024]{1,2,3,0:T(4,128)(2,1)S(1)} %copy.57), kind=kOutput, calls=%fused_computation.3.clone.1 | convolution fusion | flops 9437184 | bytes 8912896 | tf_op jit(solution)/shard_map/while/body/eval_jaxpr/csf,rsf->crf/dot_general | solution.py:98
  245.0 6.9 %copy.59 = f32[32,64,512]{2,1,0:T(8,128)} copy(f32[32,64,512]{1,0,2:T(8,128)} %add_bitcast_fusion.2) | data formatting | bytes 8388608 | tf_op jit(solution)/shard_map/while/body/eval_jaxpr/add | solution.py:96
  251.9 1.3 fusion.86
  253.2 4.9 %subtract_bitcast_fusion.2 = f32[32,64,512]{1,0,2:T(8,128)} fusion(f32[512,32,64]{2,1,0:T(8,128)S(1)} %fusion.86, bf16[64,4,512]{0,1,2:T(4,128)(2,1)S(1)} %copy-done.7, bf16[1,32,4,1024]{1,2,3,0:T(4,128)(2,1)S(1)} %copy.57), kind=kOutput, calls=%fused_computation.2.clone.1 | convolution fusion | flops 9437184 | bytes 8912896 | tf_op jit(solution)/shard_map/while/body/eval_jaxpr/csf,rsf->crf/dot_general | solution.py:101
  258.1 6.9 %copy.58 = f32[32,64,512]{2,1,0:T(8,128)} copy(f32[32,64,512]{1,0,2:T(8,128)} %subtract_bitcast_fusion.2) | data formatting | bytes 8388608 | tf_op jit(solution)/shard_map/while/body/eval_jaxpr/sub | solution.py:99
  265.1 5.8 %fusion.88 = bf16[2048,512]{1,0:T(8,128)(2,1)S(1)} fusion(bf16[1024,512]{1,0:T(8,128)(2,1)S(1)} %copy-done.2, f32[2048,512]{1,0:T(8,128)} %bitcast.74, f32[2048,512]{1,0:T(8,128)} %bitcast.73), kind=kOutput, calls=%fused_computation.6.clone.1 | convolution fusion | flops 2154823680 | bytes 11534336 | tf_op jit(solution)/shard_map/while/body/eval_jaxpr/dot_general | solution.py:103
  270.9 1.6 constant_dynamic-update-slice_fusion.2
  272.7 1.0 copy-done
  273.9 0.8 copy.57
  274.6 1.3 fusion.87
  276.0 4.9 %add_bitcast_fusion.2 = f32[32,64,512]{1,0,2:T(8,128)} fusion(f32[512,32,64]{2,1,0:T(8,128)S(1)} %fusion.87, bf16[64,4,512]{0,1,2:T(4,128)(2,1)S(1)} %copy-done.6, bf16[1,32,4,1024]{1,2,3,0:T(4,128)(2,1)S(1)} %copy.57), kind=kOutput, calls=%fused_computation.3.clone.1 | convolution fusion | flops 9437184 | bytes 8912896 | tf_op jit(solution)/shard_map/while/body/eval_jaxpr/csf,rsf->crf/dot_general | solution.py:98
  280.9 6.9 %copy.59 = f32[32,64,512]{2,1,0:T(8,128)} copy(f32[32,64,512]{1,0,2:T(8,128)} %add_bitcast_fusion.2) | data formatting | bytes 8388608 | tf_op jit(solution)/shard_map/while/body/eval_jaxpr/add | solution.py:96
  287.8 1.3 fusion.86
  289.1 4.9 %subtract_bitcast_fusion.2 = f32[32,64,512]{1,0,2:T(8,128)} fusion(f32[512,32,64]{2,1,0:T(8,128)S(1)} %fusion.86, bf16[64,4,512]{0,1,2:T(4,128)(2,1)S(1)} %copy-done.7, bf16[1,32,4,1024]{1,2,3,0:T(4,128)(2,1)S(1)} %copy.57), kind=kOutput, calls=%fused_computation.2.clone.1 | convolution fusion | flops 9437184 | bytes 8912896 | tf_op jit(solution)/shard_map/while/body/eval_jaxpr/csf,rsf->crf/dot_general | solution.py:101
  294.1 6.9 %copy.58 = f32[32,64,512]{2,1,0:T(8,128)} copy(f32[32,64,512]{1,0,2:T(8,128)} %subtract_bitcast_fusion.2) | data formatting | bytes 8388608 | tf_op jit(solution)/shard_map/while/body/eval_jaxpr/sub | solution.py:99
  301.0 5.8 %fusion.88 = bf16[2048,512]{1,0:T(8,128)(2,1)S(1)} fusion(bf16[1024,512]{1,0:T(8,128)(2,1)S(1)} %copy-done.2, f32[2048,512]{1,0:T(8,128)} %bitcast.74, f32[2048,512]{1,0:T(8,128)} %bitcast.73), kind=kOutput, calls=%fused_computation.6.clone.1 | convolution fusion | flops 2154823680 | bytes 11534336 | tf_op jit(solution)/shard_map/while/body/eval_jaxpr/dot_general | solution.py:103
  306.8 1.6 constant_dynamic-update-slice_fusion.2
  (86 shorter events, 2.6 us)
Async XLA Ops:
  6.5 151.9 %all-gather.3.cloned.1.call-start = ((), (), s32[]{:S(2)}) async-start(), calls=%async_computation | async-start | bytes 4210688 | tf_op jit(solution)/shard_map/all_gather | solution.py:80
  36.3 7.6 %copy-start.11 = (s32[64]{0:T(128)S(1)}, s32[64]{0:T(128)}, u32[]{:S(2)}) copy-start(s32[64]{0:T(128)} %param.11) | copy-start | bytes 772
  38.5 124.7 %collective-permute-start = (bf16[16,4096]{1,0:T(8,128)(2,1)S(1)}, bf16[16,4096]{1,0:T(8,128)(2,1)S(1)}, u32[]{:S(2)}, u32[]{:S(2)}) collective-permute-start(bf16[16,4096]{1,0:T(8,128)(2,1)S(1)} %slice.41), channel_id=1, source_target_pairs={{0,1},{1,2},{2,3},{3,4},{4,5},{5,6},{6,7},{7,8},{8,9},{9,10},{10,1... | collective-permute-start | bytes 393224 | tf_op jit(solution)/shard_map/ppermute | solution.py:20
  42.6 120.6 %collective-permute-start.1 = (bf16[16,4096]{1,0:T(8,128)(2,1)S(1)}, bf16[16,4096]{1,0:T(8,128)(2,1)S(1)}, u32[]{:S(2)}, u32[]{:S(2)}) collective-permute-start(bf16[16,4096]{1,0:T(8,128)(2,1)S(1)} %slice.43), channel_id=1, source_target_pairs={{1,0},{2,1},{3,2},{4,3},{5,4},{6,5},{7,6},{8,7},{9,8},{10,9},{11,1... | collective-permute-start | bytes 393224 | tf_op jit(solution)/shard_map/ppermute | solution.py:23
  133.2 2.9 copy-start.10
  133.2 2.9 copy-start.9
  133.2 3.0 copy-start.8
  163.8 1.0 copy-start.3
  164.9 1.0 copy-start
  166.8 1.3 copy-start.6
  173.1 6.9 %copy-start.4 = (bf16[64,4,512]{0,1,2:T(4,128)(2,1)S(1)}, bf16[64,4,512]{0,1,2:T(4,128)(2,1)}, u32[]{:S(2)}) copy-start(bf16[64,4,512]{0,1,2:T(4,128)(2,1)} %get-tuple-element.174) | copy-start | bytes 786436 | tf_op jit(solution)/shard_map/while
  180.0 1.3 copy-start.7
  186.2 6.9 %copy-start.2 = (bf16[1024,512]{1,0:T(8,128)(2,1)S(1)}, bf16[1024,512]{1,0:T(8,128)(2,1)}, u32[]{:S(2)}) copy-start(bf16[1024,512]{1,0:T(8,128)(2,1)} %get-tuple-element.163) | copy-start | bytes 3145732 | tf_op jit(solution)/shard_map/while
  199.0 1.6 copy-start.1
  199.0 1.8 copy-start.5
  200.8 1.0 copy-start
  202.7 1.3 copy-start.6
  209.0 6.9 %copy-start.4 = (bf16[64,4,512]{0,1,2:T(4,128)(2,1)S(1)}, bf16[64,4,512]{0,1,2:T(4,128)(2,1)}, u32[]{:S(2)}) copy-start(bf16[64,4,512]{0,1,2:T(4,128)(2,1)} %get-tuple-element.174) | copy-start | bytes 786436 | tf_op jit(solution)/shard_map/while
  215.9 1.3 copy-start.7
  222.2 6.9 %copy-start.2 = (bf16[1024,512]{1,0:T(8,128)(2,1)S(1)}, bf16[1024,512]{1,0:T(8,128)(2,1)}, u32[]{:S(2)}) copy-start(bf16[1024,512]{1,0:T(8,128)(2,1)} %get-tuple-element.163) | copy-start | bytes 3145732 | tf_op jit(solution)/shard_map/while
  234.9 1.6 copy-start.1
  234.9 1.8 copy-start.5
  236.8 1.0 copy-start
  238.7 1.3 copy-start.6
  245.0 6.9 %copy-start.4 = (bf16[64,4,512]{0,1,2:T(4,128)(2,1)S(1)}, bf16[64,4,512]{0,1,2:T(4,128)(2,1)}, u32[]{:S(2)}) copy-start(bf16[64,4,512]{0,1,2:T(4,128)(2,1)} %get-tuple-element.174) | copy-start | bytes 786436 | tf_op jit(solution)/shard_map/while
  251.9 1.3 copy-start.7
  258.1 6.9 %copy-start.2 = (bf16[1024,512]{1,0:T(8,128)(2,1)S(1)}, bf16[1024,512]{1,0:T(8,128)(2,1)}, u32[]{:S(2)}) copy-start(bf16[1024,512]{1,0:T(8,128)(2,1)} %get-tuple-element.163) | copy-start | bytes 3145732 | tf_op jit(solution)/shard_map/while
  270.9 1.6 copy-start.1
  270.9 1.8 copy-start.5
  272.7 1.0 copy-start
  274.6 1.3 copy-start.6
  280.9 6.9 %copy-start.4 = (bf16[64,4,512]{0,1,2:T(4,128)(2,1)S(1)}, bf16[64,4,512]{0,1,2:T(4,128)(2,1)}, u32[]{:S(2)}) copy-start(bf16[64,4,512]{0,1,2:T(4,128)(2,1)} %get-tuple-element.174) | copy-start | bytes 786436 | tf_op jit(solution)/shard_map/while
  287.8 1.3 copy-start.7
  294.1 6.9 %copy-start.2 = (bf16[1024,512]{1,0:T(8,128)(2,1)S(1)}, bf16[1024,512]{1,0:T(8,128)(2,1)}, u32[]{:S(2)}) copy-start(bf16[1024,512]{1,0:T(8,128)(2,1)} %get-tuple-element.163) | copy-start | bytes 3145732 | tf_op jit(solution)/shard_map/while
  306.8 1.6 copy-start.1
  306.8 1.8 copy-start.5
Sparse Core Ops, SparseCore 0:
  38.4 119.9 all-gather.2
where the time goes:
time: 316 us
  blocking collectives  88.9 us (28%)
  matrix products  80.2 us (25%)
  local copies, waits for them, and re-layouts  79.5 us (25%)
  other arithmetic  22.8 us (7%)
  between operations  21.9 us (7%)
  waiting for transfers between devices  16.6 us (5%)
  starting transfers between devices  5.32 us (2%)
    psum x1, blocking collectives, per_device(): references = lax.psum(selected, ('fibre', 'chan')).astype(jnp.bfloat16)  88.9 us
    add x4, local copies, waits for them, and re-layouts, correlate(): jnp.einsum('csf,rsf->crf', a_re, ref_re, preferred_element_type=jnp.float32)  27.7 us
    sub x4, local copies, waits for them, and re-layouts, correlate(): jnp.einsum('csf,rsf->crf', a_im, ref_re, preferred_element_type=jnp.float32)  27.7 us
    dot_general x4, matrix products, correlate(): jnp.dot(cross.reshape(group * REFS, SEG), kernel, preferred_element_type=...  23.2 us
    another operation x3, other arithmetic  20.4 us
    dot_general x4, matrix products, correlate(): jnp.einsum('csf,rsf->crf', a_re, ref_im, preferred_element_type=jnp.float32)  19.8 us
    dot_general x4, matrix products, correlate(): jnp.einsum('csf,rsf->crf', a_im, ref_im, preferred_element_type=jnp.float32)  19.8 us
    all_gather x1, waiting for transfers between devices, per_device(): piece = lax.all_gather(exported, ('fibre', 'chan'), axis=0, tiled=True)  16.6 us
  transfers between devices with their start and end apart: 3, of which 1 were waited for; matrix products, arithmetic and copies ran while one was open for 4% of the time, Pallas kernels for 0%

commit v1 on v0

--- a/solution.py
+++ b/solution.py
@@ -77,7 +77,16 @@
     )
     exported = jnp.take(flat, export_loc, axis=0)
     live = cross_mask == 1
-    piece = lax.all_gather(exported, ("fibre", "chan"), axis=0, tiled=True)
+    panels_bring = lambda u_in, axis_tag: jnp.concatenate(
+        lax.all_to_all(
+            jnp.stack(lax.axis_size(axis_tag) * [u_in]),
+            axis_name=axis_tag,
+            split_axis=0,
+            concat_axis=0,
+        ),
+        axis=0,
+    )
+    piece = panels_bring(exported, ("fibre", "chan"))
     slots = jnp.arange(piece.shape[0], dtype=jnp.int32)
     hits = (cross_ids[:, :, None] == slots[None, None, :]) & live[:, :, None]
     weights = jnp.sum(hits.astype(jnp.float32), 1).astype(jnp.bfloat16)

time: 316 us -> 337 us (1.066)
  local copies, waits for them, and re-layouts: 79.5 us -> 96.7 us
  waiting for transfers between devices: 16.6 us -> 0.01 us
  starting transfers between devices: 5.32 us -> 21 us
  between operations: 21.9 us -> 8.48 us
  other arithmetic: 22.8 us -> 35.7 us
    all_gather x1 -> x0, waiting for transfers between devices: 16.6 us -> none  [per_device(): piece = lax.all_gather(exported, ('fibre', 'chan'), axis=0, tiled=True)]
    all_to_all x0 -> x1, starting transfers between devices: none -> 15.6 us  [per_device(): lax.all_to_all(jnp.stack(lax.axis_size(axis_tag) * [u_in]), axis_name=axi...]
    another operation x3 -> x4, other arithmetic: 20.4 us -> 33.9 us
    unnamed x12 -> x18, local copies, waits for them, and re-layouts: 2.5 us -> 12 us
    another operation x0 -> x2, local copies, waits for them, and re-layouts: none -> 6.78 us  [per_device(): jnp.stack(lax.axis_size(axis_tag) * [u_in])]
  transfers between devices with their start and end apart: 3 -> 3, of which waited for: 1 -> 0; matrix products, arithmetic and copies ran while one was open for 4% -> 7% of each run, Pallas kernels for 0% -> 0%
where the time goes in v1:
time: 337 us; the launch traced here: 336 us
  local copies, waits for them, and re-layouts  96.7 us (29%)
  blocking collectives  91 us (27%)
  matrix products  82.5 us (24%)
  other arithmetic  35.7 us (11%)
  starting transfers between devices  21 us (6%)
  between operations  8.48 us (3%)
    psum x1, blocking collectives, per_device(): references = lax.psum(selected, ('fibre', 'chan')).astype(jnp.bfloat16)  91 us
    sub x4, local copies, waits for them, and re-layouts, correlate(): jnp.einsum('csf,rsf->crf', a_im, ref_re, preferred_element_type=jnp.float32)  27.7 us
    add x4, local copies, waits for them, and re-layouts, correlate(): jnp.einsum('csf,rsf->crf', a_re, ref_re, preferred_element_type=jnp.float32)  27.5 us
    dot_general x4, matrix products, correlate(): jnp.dot(cross.reshape(group * REFS, SEG), kernel, preferred_element_type=...  23.2 us
    another operation x3, other arithmetic  20.4 us
    dot_general x4, matrix products, correlate(): jnp.einsum('csf,rsf->crf', a_im, ref_im, preferred_element_type=jnp.float32)  19.7 us
    dot_general x4, matrix products, correlate(): jnp.einsum('csf,rsf->crf', a_re, ref_im, preferred_element_type=jnp.float32)  19.7 us
    all_to_all x1, starting transfers between devices, per_device(): lax.all_to_all(jnp.stack(lax.axis_size(axis_tag) * [u_in]), axis_name=axi...  15.6 us
  transfers between devices with their start and end apart: 3, of which 0 were waited for; matrix products, arithmetic and copies ran while one was open for 7% of the time, Pallas kernels for 0%

profile of v1, /device:TPU:1, one launch (start us, length us, event | category | flops | bytes accessed | tf_op | source)
XLA Modules:
  0.0 335.7 jit_solution(6123629360542432113)
XLA Ops:
  0.0 1.5 fusion.53
  6.5 8.0 %negate_convert_fusion = bf16[1024,512]{1,0:T(8,128)(2,1)S(1)} fusion(), kind=kLoop, calls=%fused_computation.36 | loop fusion | flops 8388608 | bytes 1048576 | tf_op jit(solution)/shard_map/convert.3
  17.0 1.9 dynamic-slice_bitcast_fusion.3
  19.0 0.8 copy.42
  20.2 7.9 %multiply_convert_fusion = bf16[1024,512]{1,0:T(8,128)(2,1)S(1)} fusion(f32[512]{0:T(512)S(1)} %fusion.48), kind=kLoop, calls=%fused_computation.37 | loop fusion | flops 8388608 | bytes 1050624 | tf_op jit(solution)/shard_map/convert.2
  28.1 1.3 multiply_reduce_fusion
  31.2 6.3 %stack.17 = bf16[256,1,4096]{2,1,0:T(2,128)(2,1)} broadcast(bf16[4096]{0:T(1024)(128)(2,1)S(1)} %fusion.46), dimensions={2} | broadcast | bytes 2105344 | tf_op jit(solution)/shard_map/stack | solution.py:82
  38.0 13.5 %reduce.2 = bf16[256,4096]{1,0:T(8,128)(2,1)S(1)} reduce(bf16[256,1,4096]{2,1,0:T(2,128)(2,1)} %stack.17, bf16[]{:T(256)} %broadcast.109), dimensions={1}, to_apply=%stack.17.reduce_sub_computation | reduce | bytes 4194306 | tf_op jit(solution)/shard_map/stack | solution.py:82
  51.5 2.8 reshape.97
  54.2 15.6 %all-to-all-start = ((bf16[256,2,2048]{2,1,0:T(2,128)(2,1)}), bf16[256,2,2048]{2,1,0:T(2,128)(2,1)S(1)}, u32[]{:S(2)}, u32[]{:S(2)}) async-start(bf16[256,2,2048]{2,1,0:T(2,128)(2,1)} %reshape.97), calls=%async_computation | async-start | bytes 4194304 | tf_op jit(solution)/shard_map/all_to_all | solution.py:81
  70.0 3.9 %collective-permute-start = (bf16[16,4096]{1,0:T(8,128)(2,1)S(1)}, bf16[16,4096]{1,0:T(8,128)(2,1)}, u32[]{:S(2)}, u32[]{:S(2)}) collective-permute-start(bf16[16,4096]{1,0:T(8,128)(2,1)S(1)} %slice.41), channel_id=1, source_target_pairs={{0,1},{1,2},{2,3},{3,4},{4,5},{5,6},{6,7},{7,8},{8,9},{9,10},{10,1... | collective-permute-start | bytes 393224 | tf_op jit(solution)/shard_map/ppermute | solution.py:20
  74.0 1.5 collective-permute-start.1
  75.5 1.6 fusion.45
  77.1 91.0 %all-reduce.1 = bf16[64,4096]{1,0:T(8,128)(2,1)} all-reduce(f32[64,4096]{1,0:T(8,128)S(1)} %fusion.45), channel_id=1, replica_groups=mesh['fibre'=2,'chan'=128] {'fibre','chan'}, use_global_device_ids=true, to_apply=%region_4.5 | all-reduce | flops 262144 | bytes 1572864 | tf_op jit(solution)/shard_map/psum | solution.py:65
  168.1 1.5 reshape.68
  169.7 1.1 copy.48
  170.9 1.1 copy.49
  172.3 4.5 %multiply_convert_fusion.2 = (bf16[512,512]{1,0:T(8,128)(2,1)S(1)}, bf16[512,512]{1,0:T(8,128)(2,1)S(1)}) fusion(s32[512]{0:T(512)S(1)} %iota_add_fusion), kind=kLoop, calls=%fused_computation.55 | loop fusion | flops 4980736 | bytes 1050624 | tf_op jit(solution)/shard_map/convert
  176.8 1.0 pad_maximum_fusion.1
  177.8 6.7 %reshape.98 = bf16[256,1,4096]{2,1,0:T(2,128)(2,1)} reshape(bf16[256,2,2048]{2,1,0:T(2,128)(2,1)S(1)} %all-to-all-done) | data formatting | bytes 4194304
  184.6 4.8 %fusion.25 = f32[128,4096]{1,0:T(8,128)S(1)} fusion(bf16[256,1,4096]{2,1,0:T(2,128)(2,1)} %reshape.98, bf16[128,256]{1,0:T(8,128)(2,1)S(1)} %convert_reduce_fusion.1), kind=kOutput, calls=%fused_computation.31 | convolution fusion | flops 268435456 | bytes 4259840 | tf_op jit(solution)/shard_map/dot_general | solution.py:93
  189.4 1.6 fusion.17
  191.0 0.8 reshape.67
  192.1 143.6 %while.11 = (s32[]{:T(128)}, bf16[4,32,64,512]{3,2,1,0:T(8,128)(2,1)}, bf16[4,32,4,1024]{3,2,1,0:T(4,128)(2,1)S(1)}, bf16[64,4,512]{0,1,2:T(4,128)(2,1)S(1)}, bf...) while((s32[]{:T(128)}, ...), condition=%wide.region_6.7_spmd, body=%wide.region_5.6_spmd.sunk | while | flops 2190475264 | bytes 77595424 | solution.py:115
  192.1 1.0 copy-done
  193.2 0.8 copy.57
  194.0 1.3 fusion.87
  195.3 4.9 %add_bitcast_fusion.2 = f32[32,64,512]{1,0,2:T(8,128)} fusion(f32[512,32,64]{2,1,0:T(8,128)S(1)} %fusion.87, bf16[64,4,512]{0,1,2:T(4,128)(2,1)S(1)} %copy-done.8, bf16[1,32,4,1024]{1,2,3,0:T(4,128)(2,1)S(1)} %copy.57), kind=kOutput, calls=%fused_computation.3.clone.1 | convolution fusion | flops 9437184 | bytes 8912896 | tf_op jit(solution)/shard_map/while/body/eval_jaxpr/csf,rsf->crf/dot_general | solution.py:107
  200.2 6.9 %copy.59 = f32[32,64,512]{2,1,0:T(8,128)} copy(f32[32,64,512]{1,0,2:T(8,128)} %add_bitcast_fusion.2) | data formatting | bytes 8388608 | tf_op jit(solution)/shard_map/while/body/eval_jaxpr/add | solution.py:105
  207.1 1.3 fusion.86
  208.4 4.9 %subtract_bitcast_fusion.2 = f32[32,64,512]{1,0,2:T(8,128)} fusion(f32[512,32,64]{2,1,0:T(8,128)S(1)} %fusion.86, bf16[64,4,512]{0,1,2:T(4,128)(2,1)S(1)} %copy-done.9, bf16[1,32,4,1024]{1,2,3,0:T(4,128)(2,1)S(1)} %copy.57), kind=kOutput, calls=%fused_computation.2.clone.1 | convolution fusion | flops 9437184 | bytes 8912896 | tf_op jit(solution)/shard_map/while/body/eval_jaxpr/csf,rsf->crf/dot_general | solution.py:110
  213.4 6.9 %copy.58 = f32[32,64,512]{2,1,0:T(8,128)} copy(f32[32,64,512]{1,0,2:T(8,128)} %subtract_bitcast_fusion.2) | data formatting | bytes 8388608 | tf_op jit(solution)/shard_map/while/body/eval_jaxpr/sub | solution.py:108
  220.3 5.8 %fusion.88 = bf16[2048,512]{1,0:T(8,128)(2,1)S(1)} fusion(bf16[1024,512]{1,0:T(8,128)(2,1)S(1)} %copy-done.4, f32[2048,512]{1,0:T(8,128)} %bitcast.72, f32[2048,512]{1,0:T(8,128)} %bitcast.71), kind=kOutput, calls=%fused_computation.6.clone.1 | convolution fusion | flops 2154823680 | bytes 11534336 | tf_op jit(solution)/shard_map/while/body/eval_jaxpr/dot_general | solution.py:112
  226.1 1.6 constant_dynamic-update-slice_fusion.2
  228.0 1.0 copy-done
  229.1 0.8 copy.57
  229.9 1.3 fusion.87
  231.2 4.9 %add_bitcast_fusion.2 = f32[32,64,512]{1,0,2:T(8,128)} fusion(f32[512,32,64]{2,1,0:T(8,128)S(1)} %fusion.87, bf16[64,4,512]{0,1,2:T(4,128)(2,1)S(1)} %copy-done.8, bf16[1,32,4,1024]{1,2,3,0:T(4,128)(2,1)S(1)} %copy.57), kind=kOutput, calls=%fused_computation.3.clone.1 | convolution fusion | flops 9437184 | bytes 8912896 | tf_op jit(solution)/shard_map/while/body/eval_jaxpr/csf,rsf->crf/dot_general | solution.py:107
  236.1 6.9 %copy.59 = f32[32,64,512]{2,1,0:T(8,128)} copy(f32[32,64,512]{1,0,2:T(8,128)} %add_bitcast_fusion.2) | data formatting | bytes 8388608 | tf_op jit(solution)/shard_map/while/body/eval_jaxpr/add | solution.py:105
  243.0 1.3 fusion.86
  244.3 4.9 %subtract_bitcast_fusion.2 = f32[32,64,512]{1,0,2:T(8,128)} fusion(f32[512,32,64]{2,1,0:T(8,128)S(1)} %fusion.86, bf16[64,4,512]{0,1,2:T(4,128)(2,1)S(1)} %copy-done.9, bf16[1,32,4,1024]{1,2,3,0:T(4,128)(2,1)S(1)} %copy.57), kind=kOutput, calls=%fused_computation.2.clone.1 | convolution fusion | flops 9437184 | bytes 8912896 | tf_op jit(solution)/shard_map/while/body/eval_jaxpr/csf,rsf->crf/dot_general | solution.py:110
  249.3 6.9 %copy.58 = f32[32,64,512]{2,1,0:T(8,128)} copy(f32[32,64,512]{1,0,2:T(8,128)} %subtract_bitcast_fusion.2) | data formatting | bytes 8388608 | tf_op jit(solution)/shard_map/while/body/eval_jaxpr/sub | solution.py:108
  256.2 5.8 %fusion.88 = bf16[2048,512]{1,0:T(8,128)(2,1)S(1)} fusion(bf16[1024,512]{1,0:T(8,128)(2,1)S(1)} %copy-done.4, f32[2048,512]{1,0:T(8,128)} %bitcast.72, f32[2048,512]{1,0:T(8,128)} %bitcast.71), kind=kOutput, calls=%fused_computation.6.clone.1 | convolution fusion | flops 2154823680 | bytes 11534336 | tf_op jit(solution)/shard_map/while/body/eval_jaxpr/dot_general | solution.py:112
  262.0 1.6 constant_dynamic-update-slice_fusion.2
  263.9 1.0 copy-done
  265.0 0.8 copy.57
  265.8 1.3 fusion.87
  267.1 4.9 %add_bitcast_fusion.2 = f32[32,64,512]{1,0,2:T(8,128)} fusion(f32[512,32,64]{2,1,0:T(8,128)S(1)} %fusion.87, bf16[64,4,512]{0,1,2:T(4,128)(2,1)S(1)} %copy-done.8, bf16[1,32,4,1024]{1,2,3,0:T(4,128)(2,1)S(1)} %copy.57), kind=kOutput, calls=%fused_computation.3.clone.1 | convolution fusion | flops 9437184 | bytes 8912896 | tf_op jit(solution)/shard_map/while/body/eval_jaxpr/csf,rsf->crf/dot_general | solution.py:107
  272.0 6.9 %copy.59 = f32[32,64,512]{2,1,0:T(8,128)} copy(f32[32,64,512]{1,0,2:T(8,128)} %add_bitcast_fusion.2) | data formatting | bytes 8388608 | tf_op jit(solution)/shard_map/while/body/eval_jaxpr/add | solution.py:105
  278.9 1.3 fusion.86
  280.2 4.9 %subtract_bitcast_fusion.2 = f32[32,64,512]{1,0,2:T(8,128)} fusion(f32[512,32,64]{2,1,0:T(8,128)S(1)} %fusion.86, bf16[64,4,512]{0,1,2:T(4,128)(2,1)S(1)} %copy-done.9, bf16[1,32,4,1024]{1,2,3,0:T(4,128)(2,1)S(1)} %copy.57), kind=kOutput, calls=%fused_computation.2.clone.1 | convolution fusion | flops 9437184 | bytes 8912896 | tf_op jit(solution)/shard_map/while/body/eval_jaxpr/csf,rsf->crf/dot_general | solution.py:110
  285.2 6.9 %copy.58 = f32[32,64,512]{2,1,0:T(8,128)} copy(f32[32,64,512]{1,0,2:T(8,128)} %subtract_bitcast_fusion.2) | data formatting | bytes 8388608 | tf_op jit(solution)/shard_map/while/body/eval_jaxpr/sub | solution.py:108
  292.1 5.8 %fusion.88 = bf16[2048,512]{1,0:T(8,128)(2,1)S(1)} fusion(bf16[1024,512]{1,0:T(8,128)(2,1)S(1)} %copy-done.4, f32[2048,512]{1,0:T(8,128)} %bitcast.72, f32[2048,512]{1,0:T(8,128)} %bitcast.71), kind=kOutput, calls=%fused_computation.6.clone.1 | convolution fusion | flops 2154823680 | bytes 11534336 | tf_op jit(solution)/shard_map/while/body/eval_jaxpr/dot_general | solution.py:112
  297.9 1.6 constant_dynamic-update-slice_fusion.2
  299.8 1.0 copy-done
  300.9 0.8 copy.57
  301.7 1.3 fusion.87
  303.0 4.9 %add_bitcast_fusion.2 = f32[32,64,512]{1,0,2:T(8,128)} fusion(f32[512,32,64]{2,1,0:T(8,128)S(1)} %fusion.87, bf16[64,4,512]{0,1,2:T(4,128)(2,1)S(1)} %copy-done.8, bf16[1,32,4,1024]{1,2,3,0:T(4,128)(2,1)S(1)} %copy.57), kind=kOutput, calls=%fused_computation.3.clone.1 | convolution fusion | flops 9437184 | bytes 8912896 | tf_op jit(solution)/shard_map/while/body/eval_jaxpr/csf,rsf->crf/dot_general | solution.py:107
  307.9 6.9 %copy.59 = f32[32,64,512]{2,1,0:T(8,128)} copy(f32[32,64,512]{1,0,2:T(8,128)} %add_bitcast_fusion.2) | data formatting | bytes 8388608 | tf_op jit(solution)/shard_map/while/body/eval_jaxpr/add | solution.py:105
  314.8 1.3 fusion.86
  316.1 4.9 %subtract_bitcast_fusion.2 = f32[32,64,512]{1,0,2:T(8,128)} fusion(f32[512,32,64]{2,1,0:T(8,128)S(1)} %fusion.86, bf16[64,4,512]{0,1,2:T(4,128)(2,1)S(1)} %copy-done.9, bf16[1,32,4,1024]{1,2,3,0:T(4,128)(2,1)S(1)} %copy.57), kind=kOutput, calls=%fused_computation.2.clone.1 | convolution fusion | flops 9437184 | bytes 8912896 | tf_op jit(solution)/shard_map/while/body/eval_jaxpr/csf,rsf->crf/dot_general | solution.py:110
  321.1 6.9 %copy.58 = f32[32,64,512]{2,1,0:T(8,128)} copy(f32[32,64,512]{1,0,2:T(8,128)} %subtract_bitcast_fusion.2) | data formatting | bytes 8388608 | tf_op jit(solution)/shard_map/while/body/eval_jaxpr/sub | solution.py:108
  328.0 5.8 %fusion.88 = bf16[2048,512]{1,0:T(8,128)(2,1)S(1)} fusion(bf16[1024,512]{1,0:T(8,128)(2,1)S(1)} %copy-done.4, f32[2048,512]{1,0:T(8,128)} %bitcast.72, f32[2048,512]{1,0:T(8,128)} %bitcast.71), kind=kOutput, calls=%fused_computation.6.clone.1 | convolution fusion | flops 2154823680 | bytes 11534336 | tf_op jit(solution)/shard_map/while/body/eval_jaxpr/dot_general | solution.py:112
  333.8 1.6 constant_dynamic-update-slice_fusion.2
  (94 shorter events, 4.5 us)
Async XLA Ops:
  30.4 7.0 %copy-start.2 = (bf16[128,4096]{1,0:T(8,128)(2,1)}, bf16[128,4096]{1,0:T(8,128)(2,1)S(1)}, u32[]{:S(2)}) copy-start(bf16[128,4096]{1,0:T(8,128)(2,1)S(1)} %reshape.65) | copy-start | bytes 3145732
  54.2 21.3 %copy-start.13 = (s32[64]{0:T(128)S(1)}, s32[64]{0:T(128)}, u32[]{:S(2)}) copy-start(s32[64]{0:T(128)} %param.11) | copy-start | bytes 772
  54.2 123.6 %all-to-all-start = ((bf16[256,2,2048]{2,1,0:T(2,128)(2,1)}), bf16[256,2,2048]{2,1,0:T(2,128)(2,1)S(1)}, u32[]{:S(2)}, u32[]{:S(2)}) async-start(bf16[256,2,2048]{2,1,0:T(2,128)(2,1)} %reshape.97), calls=%async_computation | async-start | bytes 4194304 | tf_op jit(solution)/shard_map/all_to_all | solution.py:81
  70.0 119.4 %collective-permute-start = (bf16[16,4096]{1,0:T(8,128)(2,1)S(1)}, bf16[16,4096]{1,0:T(8,128)(2,1)}, u32[]{:S(2)}, u32[]{:S(2)}) collective-permute-start(bf16[16,4096]{1,0:T(8,128)(2,1)S(1)} %slice.41), channel_id=1, source_target_pairs={{0,1},{1,2},{2,3},{3,4},{4,5},{5,6},{6,7},{7,8},{8,9},{9,10},{10,1... | collective-permute-start | bytes 393224 | tf_op jit(solution)/shard_map/ppermute | solution.py:20
  74.0 115.4 %collective-permute-start.1 = (bf16[16,4096]{1,0:T(8,128)(2,1)S(1)}, bf16[16,4096]{1,0:T(8,128)(2,1)}, u32[]{:S(2)}, u32[]{:S(2)}) collective-permute-start(bf16[16,4096]{1,0:T(8,128)(2,1)S(1)} %slice.43), channel_id=1, source_target_pairs={{1,0},{2,1},{3,2},{4,3},{5,4},{6,5},{7,6},{8,7},{9,8},{10,9},{11,1... | collective-permute-start | bytes 393224 | tf_op jit(solution)/shard_map/ppermute | solution.py:23
  168.1 3.9 %copy-start.12 = (s32[128,2]{0,1:T(2,128)S(1)}, s32[128,2]{0,1:T(2,128)}, u32[]{:S(2)}) copy-start(s32[128,2]{0,1:T(2,128)} %param.14) | copy-start | bytes 3076
  168.1 4.0 %copy-start.11 = (s32[128,2]{0,1:T(2,128)S(1)}, s32[128,2]{0,1:T(2,128)}, u32[]{:S(2)}) copy-start(s32[128,2]{0,1:T(2,128)} %param.13) | copy-start | bytes 3076
  168.1 4.1 %copy-start.10 = (s32[128,8]{0,1:T(8,128)S(1)}, s32[128,8]{0,1:T(8,128)}, u32[]{:S(2)}) copy-start(s32[128,8]{0,1:T(8,128)} %param.12) | copy-start | bytes 12292
  184.6 4.8 %copy-start.3 = (bf16[128,4096]{1,0:T(8,128)(2,1)S(1)}, bf16[128,4096]{1,0:T(8,128)(2,1)}, u32[]{:S(2)}) copy-start(bf16[128,4096]{1,0:T(8,128)(2,1)} %copy-done.2) | copy-start | bytes 3145732
  191.0 1.0 copy-start.5
  192.1 1.0 copy-start
  194.0 1.3 copy-start.8
  200.2 6.9 %copy-start.6 = (bf16[64,4,512]{0,1,2:T(4,128)(2,1)S(1)}, bf16[64,4,512]{0,1,2:T(4,128)(2,1)}, u32[]{:S(2)}) copy-start(bf16[64,4,512]{0,1,2:T(4,128)(2,1)} %get-tuple-element.175) | copy-start | bytes 786436 | tf_op jit(solution)/shard_map/while
  207.1 1.3 copy-start.9
  213.4 6.9 %copy-start.4 = (bf16[1024,512]{1,0:T(8,128)(2,1)S(1)}, bf16[1024,512]{1,0:T(8,128)(2,1)}, u32[]{:S(2)}) copy-start(bf16[1024,512]{1,0:T(8,128)(2,1)} %get-tuple-element.163) | copy-start | bytes 3145732 | tf_op jit(solution)/shard_map/while
  226.1 1.6 copy-start.1
  226.1 1.8 copy-start.7
  228.0 1.0 copy-start
  229.9 1.3 copy-start.8
  236.1 6.9 %copy-start.6 = (bf16[64,4,512]{0,1,2:T(4,128)(2,1)S(1)}, bf16[64,4,512]{0,1,2:T(4,128)(2,1)}, u32[]{:S(2)}) copy-start(bf16[64,4,512]{0,1,2:T(4,128)(2,1)} %get-tuple-element.175) | copy-start | bytes 786436 | tf_op jit(solution)/shard_map/while
  243.0 1.3 copy-start.9
  249.3 6.9 %copy-start.4 = (bf16[1024,512]{1,0:T(8,128)(2,1)S(1)}, bf16[1024,512]{1,0:T(8,128)(2,1)}, u32[]{:S(2)}) copy-start(bf16[1024,512]{1,0:T(8,128)(2,1)} %get-tuple-element.163) | copy-start | bytes 3145732 | tf_op jit(solution)/shard_map/while
  262.0 1.6 copy-start.1
  262.0 1.8 copy-start.7
  263.9 1.0 copy-start
  265.8 1.3 copy-start.8
  272.0 6.9 %copy-start.6 = (bf16[64,4,512]{0,1,2:T(4,128)(2,1)S(1)}, bf16[64,4,512]{0,1,2:T(4,128)(2,1)}, u32[]{:S(2)}) copy-start(bf16[64,4,512]{0,1,2:T(4,128)(2,1)} %get-tuple-element.175) | copy-start | bytes 786436 | tf_op jit(solution)/shard_map/while
  278.9 1.3 copy-start.9
  285.2 6.9 %copy-start.4 = (bf16[1024,512]{1,0:T(8,128)(2,1)S(1)}, bf16[1024,512]{1,0:T(8,128)(2,1)}, u32[]{:S(2)}) copy-start(bf16[1024,512]{1,0:T(8,128)(2,1)} %get-tuple-element.163) | copy-start | bytes 3145732 | tf_op jit(solution)/shard_map/while
  297.9 1.6 copy-start.1
  297.9 1.8 copy-start.7
  299.8 1.0 copy-start
  301.7 1.3 copy-start.8
  307.9 6.9 %copy-start.6 = (bf16[64,4,512]{0,1,2:T(4,128)(2,1)S(1)}, bf16[64,4,512]{0,1,2:T(4,128)(2,1)}, u32[]{:S(2)}) copy-start(bf16[64,4,512]{0,1,2:T(4,128)(2,1)} %get-tuple-element.175) | copy-start | bytes 786436 | tf_op jit(solution)/shard_map/while
  314.8 1.3 copy-start.9
  321.1 6.9 %copy-start.4 = (bf16[1024,512]{1,0:T(8,128)(2,1)S(1)}, bf16[1024,512]{1,0:T(8,128)(2,1)}, u32[]{:S(2)}) copy-start(bf16[1024,512]{1,0:T(8,128)(2,1)} %get-tuple-element.163) | copy-start | bytes 3145732 | tf_op jit(solution)/shard_map/while
  333.8 1.6 copy-start.1
  333.8 1.8 copy-start.7
